TPU v7x, 256 devices: a whole 4x4x8 slice. The times are simulated.
256 devices in a mesh: tensor: 8 (over x, core), req: 32 (over y, z).
Axes of the slice: x: 4, y: 4, z: 8, core: 2. Of those that a mesh axis runs over, the one named last changes fastest.
Arguments:
- attention_output: bfloat16 [16384, 4096], P('req', 'tensor'), may hold values from -6 to 6
- residual: bfloat16 [16384, 8192], P('req', 'tensor'), may hold values from -6 to 6
- projection_weight: bfloat16 [4096, 8192], P('tensor'), may hold values from -0.09375 to 0.09375
- adapter_down_maps: bfloat16 [256, 4096, 64], P('req', 'tensor'), may hold values from -0.09375 to 0.09375
- adapter_up_maps: bfloat16 [256, 64, 8192], P('req', None, 'tensor'), may hold values from -0.75 to 0.75
- adapter_pool_slot: int32 [256], replicated, may hold values from 0 to 255, as said below
- request_adapter_id: int32 [32, 32], replicated, may hold values from 0 to 255, as said below
- request_token_length: int32 [32, 32], P('req'), may hold values from 1 to 32, 512 in all within a row
Outputs:
- mixed: bfloat16 [16384, 8192], P('req', 'tensor')
Inputs may be any that keep to these rules, and one draw needn't show every extreme that they name: `adapter_pool_slot`: each slot appears once; the slot s lies on index s // 8 of req, its owner. `request_adapter_id`: the 32 requests of one group use adapters with 32 distinct owners. `request_token_length`: each group's lengths sum to 512; in each group the largest is exactly 32.
All inputs are finite; a program needn't handle non-finite values.
Results may differ from a plain program's by a relative error of at most 0.014.
Values may be sent and summed in bfloat16 or wider, within the bound.
No kernel may reach another device: no remote copies, remote signals or barrier semaphores. Data moves between devices by JAX's collectives and lax.ppermute only.
A program may use at most 128 MiB of HBM per device.

v0:
```python
import jax
import jax.numpy as jnp
from jax import lax
from jax.sharding import PartitionSpec as P


def per_device(
    attention_output,
    residual,
    projection_weight,
    adapter_down_maps,
    adapter_up_maps,
    adapter_pool_slot,
    request_adapter_id,
    request_token_length,
):
    groups = lax.axis_size("req")
    me_index = lax.axis_index("req")
    tok_rows = attention_output.shape[0]
    features = attention_output.shape[1]
    pooled_adapter_rows = adapter_down_maps.shape[0]
    lengths = request_token_length[0]
    requests = lengths.shape[0]
    ends = jnp.cumsum(lengths)
    starts = ends - lengths
    my_ids = lax.dynamic_index_in_dim(request_adapter_id, me_index, 0, keepdims=False)
    my_owner = jnp.take(adapter_pool_slot, my_ids) // pooled_adapter_rows
    positions = jnp.arange(tok_rows, dtype=jnp.int32)
    tok_req = jnp.sum((positions[:, None] >= ends[None, :]).astype(jnp.int32), 1)
    req_hot = tok_req[:, None] == jnp.arange(requests, dtype=jnp.int32)[None, :]
    tok_owner = jnp.sum(jnp.where(req_hot, my_owner[None, :], 0), 1)
    tok_start = jnp.sum(jnp.where(req_hot, starts[None, :], 0), 1)
    all_slots = jnp.take(adapter_pool_slot, request_adapter_id)
    mine = all_slots // pooled_adapter_rows == me_index
    block_row_index = jnp.sum(jnp.where(mine, all_slots % pooled_adapter_rows, 0), 1)
    selected_down_map = jnp.take(adapter_down_maps, block_row_index, axis=0)
    selected_up_map = jnp.take(adapter_up_maps, block_row_index, axis=0)
    most_rows = 2 * tok_rows // requests
    owner_hot = my_owner[None, :] == jnp.arange(groups, dtype=jnp.int32)[:, None]
    first = jnp.sum(jnp.where(owner_hot, starts[None, :], 0), 1)
    count = jnp.sum(jnp.where(owner_hot, lengths[None, :], 0), 1)
    slot_pos = jnp.arange(most_rows, dtype=jnp.int32)
    source = first[:, None] + slot_pos[None, :]
    valid = slot_pos[None, :] < count[:, None]
    padded = jnp.concatenate([attention_output, jnp.zeros((1, features), jnp.bfloat16)], 0)
    outgoing = jnp.take(padded, jnp.where(valid, source, tok_rows), axis=0)
    partial_value = jnp.dot(attention_output, projection_weight, preferred_element_type=jnp.float32)
    base = lax.psum_scatter(
        partial_value.astype(jnp.bfloat16), "tensor", scatter_dimension=1, tiled=True
    ).astype(jnp.float32)
    reduced_rows = jnp.einsum(
        "sdy,syj->sdj",
        lax.all_to_all(outgoing, "req", split_axis=0, concat_axis=0, tiled=True),
        selected_down_map,
        preferred_element_type=jnp.float32,
    )
    reduced_rows = lax.psum(reduced_rows.astype(jnp.bfloat16), "tensor").astype(jnp.float32)
    raised_output = jnp.einsum(
        "iut,itb->iub",
        reduced_rows.astype(jnp.bfloat16),
        selected_up_map,
        preferred_element_type=jnp.float32,
    )
    returned = lax.all_to_all(
        raised_output.astype(jnp.bfloat16), "req", split_axis=0, concat_axis=0, tiled=True
    ).astype(raised_output.dtype)
    flat = returned.reshape(groups * most_rows, returned.shape[2])
    delta = jnp.take(flat, tok_owner * most_rows + positions - tok_start, axis=0)
    return (residual.astype(jnp.float32) + base + delta).astype(jnp.bfloat16)


def solution(mesh):
    in_specs = (
        P("req", "tensor"),
        P("req", "tensor"),
        P("tensor", None),
        P("req", "tensor", None),
        P("req", None, "tensor"),
        P(),
        P(),
        P("req", None),
    )
    out_specs = P("req", "tensor")
    return jax.shard_map(
        per_device, mesh=mesh, in_specs=in_specs, out_specs=out_specs, check_vma=False
    )
```

profile of v0, /device:TPU:6, one launch (start us, length us, event | category | flops | bytes accessed | tf_op | source)
XLA Modules:
  0.0 203.0 jit_solution(16693608785722491008)
XLA Ops:
  6.5 0.0 copy-start
  6.5 0.8 fusion.22
  7.3 0.7 copy.11
  8.1 0.1 reduce-window.4
  8.1 0.1 reduce
  8.2 1.4 gather_fusion
  9.6 0.7 fusion.24
  10.3 0.8 select_reduce_fusion.3
  11.1 0.1 fusion.19
  11.2 0.1 compare_select_fusion.1
  11.3 0.1 reshape.232
  11.4 1.1 concatenate.3
  12.5 4.0 %gather_fusion.1 = bf16[1024,512]{1,0:T(8,128)(2,1)S(1)} fusion(bf16[513,512]{1,0:T(8,128)(2,1)S(1)} %concatenate.3, s32[1024]{0:T(1024)S(1)} %broadcast_clamp_fusion), kind=kCustom, calls=%fused_computation.1 | custom fusion | bytes 2101248 | tf_op jit(solution)/shard_map/jit(_take)/gather | solution.py:46
  16.4 0.0 copy-start.4
  16.4 0.0 copy-start.1
  16.5 1.2 broadcast_select_fusion
  17.6 11.5 %all-to-all-start = ((bf16[32,32,512]{2,1,0:T(8,128)(2,1)}), bf16[32,32,512]{2,1,0:T(8,128)(2,1)S(1)}, u32[]{:S(2)}, u32[]{:S(2)}) async-start(bf16[32,32,512]{2,1,0:T(8,128)(2,1)} %broadcast_select_fusion), calls=%async_computation.1 | async-start | bytes 2097152 | tf_op jit(solution)/shard_map/all_to_all | solution.py:53
  29.1 0.0 all-reduce.3.cloned.1.call-start
  29.2 0.0 copy-done.4
  29.2 0.1 reshape.240
  29.3 0.0 copy-done.1
  29.3 0.0 copy-start.2
  29.3 6.8 %gather_fusion.2 = s32[1024]{0:T(1024)S(1)} fusion(s32[256]{0:T(256)S(1)} %copy-done.1, s32[1024]{0:T(1024)S(1)} %broadcast_clamp_fusion.1), kind=kCustom, calls=%fused_computation.2 | custom fusion | bytes 12288 | tf_op jit(solution)/shard_map/jit(_take)/gather | solution.py:33
  36.1 0.1 reshape.239
  36.2 0.1 fusion.16
  36.4 0.0 copy-done.2
  36.4 2.0 %gather_fusion.3 = bf16[32,512,64]{1,2,0:T(8,128)(2,1)} fusion(bf16[8,512,64]{1,2,0:T(8,128)(2,1)S(1)} %copy-done.2, s32[1024]{0:T(1024)S(1)} %pad_clamp_fusion.1), kind=kCustom, calls=%fused_computation.3 | custom fusion | bytes 4194432 | tf_op jit(solution)/shard_map/jit(_take)/gather | solution.py:36
  38.4 0.0 copy-start.3
  38.4 19.3 %all-to-all-done = bf16[32,32,512]{2,1,0:T(8,128)(2,1)S(1)} async-done(((bf16[32,32,512]{2,1,0:T(8,128)(2,1)}), bf16[32,32,512]{2,1,0:T(8,128)(2,1)S(1)}, u32[]{:S(2)}, u32[]{:S(2)}) %all-to-all-start) | async-done | bytes 1048608 | tf_op jit(solution)/shard_map/all_to_all | solution.py:53
  57.7 3.1 %fusion.10 = bf16[32,32,64]{2,1,0:T(8,128)(2,1)} fusion(bf16[32,32,512]{2,1,0:T(8,128)(2,1)S(1)} %all-to-all-done, bf16[32,512,64]{1,2,0:T(8,128)(2,1)} %gather_fusion.3, pred[32]{0:T(512)(128)(4,1)S(1)} %compare_and_fusion), kind=kOutput, calls=%fused_computation.17 | convolution fusion | flops 68222976 | bytes 3276832 | tf_op jit(solution)/shard_map/sdy,syj->sdj/dot_general | solution.py:51
  60.8 0.0 all-reduce.3.cloned.1.call-update
  60.8 0.0 reduce-scatter.2.cloned.1.call-start
  60.9 0.0 copy-done.3
  60.9 10.1 %convolution_convert_fusion = bf16[512,8192]{1,0:T(8,128)(2,1)} fusion(bf16[512,512]{1,0:T(8,128)(2,1)S(1)} %copy-done.3, bf16[512,8192]{1,0:T(8,128)(2,1)} %param.10), kind=kOutput, calls=%fused_computation.6 | convolution fusion | flops 4299161600 | bytes 17301504 | tf_op jit(solution)/shard_map/dot_general | solution.py:47
  71.0 0.0 reduce-scatter.2.cloned.1.call-update
  71.0 0.0 copy-done
  71.0 2.8 %gather_fusion.4 = bf16[32,64,1024]{2,1,0:T(8,128)(2,1)} fusion(bf16[8,64,1024]{2,1,0:T(8,128)(2,1)S(1)} %copy-done, s32[1024]{0:T(1024)S(1)} %pad_clamp_fusion.1), kind=kCustom, calls=%fused_computation.4 | custom fusion | bytes 8388736 | tf_op jit(solution)/shard_map/jit(_take)/gather | solution.py:37
  73.8 46.8 %all-reduce.3.cloned.1.call-done = bf16[32,32,64]{2,1,0:T(8,128)(2,1)} async-done(((bf16[32,32,64]{2,1,0:T(8,128)(2,1)}), bf16[32,32,64]{2,1,0:T(8,128)(2,1)}) %all-reduce.3.cloned.1.call-update) | async-done | bytes 131088 | tf_op jit(solution)/shard_map/psum | solution.py:57
  120.6 4.4 %fusion.7 = bf16[32,32,1024]{2,1,0:T(8,128)(2,1)} fusion(bf16[32,32,64]{2,1,0:T(8,128)(2,1)} %all-reduce.3.cloned.1.call-done, bf16[32,64,1024]{2,1,0:T(8,128)(2,1)} %gather_fusion.4, pred[32]{0:T(512)(128)(4,1)S(1)} %compare_and_fusion), kind=kOutput, calls=%fused_computation.16 | convolution fusion | flops 137363456 | bytes 6422560 | tf_op jit(solution)/shard_map/iut,itb->iub/dot_general | solution.py:58
  125.1 9.8 %all-to-all-start.1 = ((bf16[32,32,1024]{2,1,0:T(8,128)(2,1)}), bf16[32,32,1024]{2,1,0:T(8,128)(2,1)S(1)}, u32[]{:S(2)}, u32[]{:S(2)}) async-start(bf16[32,32,1024]{2,1,0:T(8,128)(2,1)} %fusion.7), calls=%async_computation.2 | async-start | bytes 4194304 | tf_op jit(solution)/shard_map/all_to_all | solution.py:64
  134.9 0.1 convert_reduce_fusion
  135.0 0.1 select_reduce_fusion.1
  135.2 50.4 %all-to-all-done.1 = bf16[32,32,1024]{2,1,0:T(8,128)(2,1)S(1)} async-done(((bf16[32,32,1024]{2,1,0:T(8,128)(2,1)}), bf16[32,32,1024]{2,1,0:T(8,128)(2,1)S(1)}, u32[]{:S(2)}, u32[]{:S(2)}) %all-to-all-start.1) | async-done | bytes 2097184 | tf_op jit(solution)/shard_map/all_to_all | solution.py:64
  185.6 2.6 %bitcast_convert_fusion = f32[1024,1024]{1,0:T(8,128)} fusion(bf16[32,32,1024]{2,1,0:T(8,128)(2,1)S(1)} %all-to-all-done.1), kind=kLoop, calls=%fused_computation.10 | loop fusion | flops 1048576 | bytes 6291456 | tf_op jit(solution)/shard_map/reshape | solution.py:67
  188.2 5.0 %gather_fusion.5 = f32[512,1024]{1,0:T(8,128)S(1)} fusion(f32[1024,1024]{1,0:T(8,128)} %bitcast_convert_fusion, s32[1024]{0:T(1024)S(1)} %pad_clamp_fusion), kind=kCustom, calls=%fused_computation.5 | custom fusion | bytes 4196352 | tf_op jit(solution)/shard_map/jit(_take)/gather | solution.py:68
  193.2 0.0 reduce-scatter.2.cloned.1.call-done
  193.2 2.9 %add_convert_fusion = bf16[512,1024]{1,0:T(8,128)(2,1)} fusion(f32[512,1024]{1,0:T(8,128)S(1)} %gather_fusion.5, bf16[512,1024]{1,0:T(8,128)(2,1)} %reduce-scatter.2.cloned.1.call-done, bf16[512,1024]{1,0:T(8,128)(2,1)} %param.9, pred[512]{0:T(512)(128)(4,1)S(1)} %compare_and_fusion.1), kind=kLoop, calls=%fused_computation.11 | loop fusion | flops 3145728 | bytes 5243392 | tf_op jit(solution)/shard_map/convert_element_type | solution.py:69
  (11 shorter events, 0.1 us)
Async XLA Ops:
  6.5 64.5 %copy-start = (bf16[8,64,1024]{2,1,0:T(8,128)(2,1)S(1)}, bf16[8,64,1024]{2,1,0:T(8,128)(2,1)}, u32[]{:S(2)}) copy-start(bf16[8,64,1024]{2,1,0:T(8,128)(2,1)} %param.12) | copy-start | bytes 3145732
  16.4 12.7 %copy-start.4 = (s32[32,32]{1,0:T(8,128)S(1)}, s32[32,32]{1,0:T(8,128)}, u32[]{:S(2)}) copy-start(s32[32,32]{1,0:T(8,128)} %param.14) | copy-start | bytes 12292
  16.4 12.8 %copy-start.1 = (s32[256]{0:T(256)S(1)}, s32[256]{0:T(256)}, u32[]{:S(2)}) copy-start(s32[256]{0:T(256)} %param.13) | copy-start | bytes 3076
  17.6 40.1 %all-to-all-start = ((bf16[32,32,512]{2,1,0:T(8,128)(2,1)}), bf16[32,32,512]{2,1,0:T(8,128)(2,1)S(1)}, u32[]{:S(2)}, u32[]{:S(2)}) async-start(bf16[32,32,512]{2,1,0:T(8,128)(2,1)} %broadcast_select_fusion), calls=%async_computation.1 | async-start | bytes 2097152 | tf_op jit(solution)/shard_map/all_to_all | solution.py:53
  29.1 91.5 %all-reduce.3.cloned.1.call-start = ((), (), s32[]{:S(2)}) async-start(), calls=%async_computation.4 | async-start | bytes 524288 | tf_op jit(solution)/shard_map/psum | solution.py:57
  29.3 7.1 %copy-start.2 = (bf16[8,512,64]{1,2,0:T(8,128)(2,1)S(1)}, bf16[8,512,64]{1,2,0:T(8,128)(2,1)}, u32[]{:S(2)}) copy-start(bf16[8,512,64]{1,2,0:T(8,128)(2,1)} %param.11) | copy-start | bytes 1572868
  38.4 22.5 %copy-start.3 = (bf16[512,512]{1,0:T(8,128)(2,1)S(1)}, bf16[512,512]{1,0:T(8,128)(2,1)}, u32[]{:S(2)}) copy-start(bf16[512,512]{1,0:T(8,128)(2,1)} %param.8) | copy-start | bytes 1572868
  60.8 132.4 %reduce-scatter.2.cloned.1.call-start = ((), (), s32[]{:S(2)}) async-start(), calls=%async_computation.3 | async-start | bytes 9437184 | tf_op jit(solution)/shard_map/reduce_scatter | solution.py:48
  125.1 60.5 %all-to-all-start.1 = ((bf16[32,32,1024]{2,1,0:T(8,128)(2,1)}), bf16[32,32,1024]{2,1,0:T(8,128)(2,1)S(1)}, u32[]{:S(2)}, u32[]{:S(2)}) async-start(bf16[32,32,1024]{2,1,0:T(8,128)(2,1)} %fusion.7), calls=%async_computation.2 | async-start | bytes 4194304 | tf_op jit(solution)/shard_map/all_to_all | solution.py:64
Sparse Core Ops, SparseCore 0:
  61.0 59.6 all-reduce.2
  123.2 54.4 reduce-scatter.1
where the time goes:
time: 204 us; the launch traced here: 203 us
  waiting for transfers between devices  117 us (57%)
  local copies, waits for them, and re-layouts  24.1 us (12%)
  starting transfers between devices  21.4 us (10%)
  matrix products  17.6 us (9%)
  between operations  13.6 us (7%)
  other arithmetic  9.67 us (5%)
    all_to_all x1, waiting for transfers between devices, per_device(): lax.all_to_all(raised_output.astype(jnp.bfloat16), 'req', split_axis=0, c...  50.4 us
    psum x1, waiting for transfers between devices, per_device(): lax.psum(reduced_rows.astype(jnp.bfloat16), 'tensor').astype(jnp.float32)  46.8 us
    all_to_all x1, waiting for transfers between devices, per_device(): lax.all_to_all(outgoing, 'req', split_axis=0, concat_axis=0, tiled=True)  19.3 us
    all_to_all x1, starting transfers between devices, per_device(): lax.all_to_all(outgoing, 'req', split_axis=0, concat_axis=0, tiled=True)  11.5 us
    dot_general x1, matrix products, per_device(): jnp.dot(attention_output, projection_weight, preferred_element_type=jnp.f...  10.1 us
    all_to_all x1, starting transfers between devices, per_device(): lax.all_to_all(raised_output.astype(jnp.bfloat16), 'req', split_axis=0, c...  9.85 us
    gather x2, local copies, waits for them, and re-layouts, per_device(): all_slots = jnp.take(adapter_pool_slot, request_adapter_id)  6.9 us
    gather x1, local copies, waits for them, and re-layouts, per_device(): jnp.take(flat, tok_owner * most_rows + positions - tok_start, axis=0)  5.01 us
  transfers between devices with their start and end apart: 4, of which 3 were waited for; matrix products, arithmetic and copies ran while one was open for 17% of the time, Pallas kernels for 0%

commit v1 on v0

--- a/solution.py
+++ b/solution.py
@@ -54,7 +54,9 @@
         selected_down_map,
         preferred_element_type=jnp.float32,
     )
-    reduced_rows = lax.psum(reduced_rows.astype(jnp.bfloat16), "tensor").astype(jnp.float32)
+    reduced_rows = jnp.sum(
+        lax.all_gather(reduced_rows.astype(jnp.bfloat16), "tensor"), axis=0
+    ).astype(jnp.float32)
     raised_output = jnp.einsum(
         "iut,itb->iub",
         reduced_rows.astype(jnp.bfloat16),

time: 204 us -> 170 us (0.83)
  waiting for transfers between devices: 117 us -> 79.9 us
  other arithmetic: 9.67 us -> 11.8 us
    psum x1 -> x0, waiting for transfers between devices: 46.8 us -> none  [per_device(): lax.psum(reduced_rows.astype(jnp.bfloat16), 'tensor').astype(jnp.float32)]
    all_gather x0 -> x1, waiting for transfers between devices: none -> 10.3 us  [per_device(): lax.all_gather(reduced_rows.astype(jnp.bfloat16), 'tensor')]
    reduce_sum x0 -> x1, other arithmetic: none -> 2.1 us  [per_device(): jnp.sum(lax.all_gather(reduced_rows.astype(jnp.bfloat16), 'tensor'), axis=0)]
  transfers between devices with their start and end apart: 4 -> 4, of which waited for: 3 -> 3; matrix products, arithmetic and copies ran while one was open for 17% -> 22% of each run, Pallas kernels for 0% -> 0%
where the time goes in v1:
time: 170 us; the launch traced here: 168 us
  waiting for transfers between devices  79.9 us (47%)
  local copies, waits for them, and re-layouts  24.1 us (14%)
  starting transfers between devices  21.4 us (13%)
  matrix products  17.5 us (10%)
  between operations  13.6 us (8%)
  other arithmetic  11.8 us (7%)
    all_to_all x1, waiting for transfers between devices, per_device(): lax.all_to_all(raised_output.astype(jnp.bfloat16), 'req', split_axis=0, c...  50.1 us
    all_to_all x1, waiting for transfers between devices, per_device(): lax.all_to_all(outgoing, 'req', split_axis=0, concat_axis=0, tiled=True)  19.3 us
    all_to_all x1, starting transfers between devices, per_device(): lax.all_to_all(outgoing, 'req', split_axis=0, concat_axis=0, tiled=True)  11.5 us
    all_gather x1, waiting for transfers between devices, per_device(): lax.all_gather(reduced_rows.astype(jnp.bfloat16), 'tensor')  10.3 us
    dot_general x1, matrix products, per_device(): jnp.dot(attention_output, projection_weight, preferred_element_type=jnp.f...  10.1 us
    all_to_all x1, starting transfers between devices, per_device(): lax.all_to_all(raised_output.astype(jnp.bfloat16), 'req', split_axis=0, c...  9.85 us
    gather x2, local copies, waits for them, and re-layouts, per_device(): all_slots = jnp.take(adapter_pool_slot, request_adapter_id)  6.9 us
    gather x1, local copies, waits for them, and re-layouts, per_device(): jnp.take(flat, tok_owner * most_rows + positions - tok_start, axis=0)  5.01 us
  transfers between devices with their start and end apart: 4, of which 3 were waited for; matrix products, arithmetic and copies ran while one was open for 22% of the time, Pallas kernels for 0%

profile of v1, /device:TPU:6, one launch (start us, length us, event | category | flops | bytes accessed | tf_op | source)
XLA Modules:
  0.0 168.2 jit_solution(7750403156298052978)
XLA Ops:
  6.5 0.0 copy-start
  6.5 0.8 fusion.22
  7.3 0.7 copy.12
  8.1 0.1 reduce-window.4
  8.1 0.1 reduce.1
  8.2 1.4 gather_fusion
  9.6 0.7 fusion.24
  10.3 0.8 select_reduce_fusion.3
  11.1 0.1 fusion.19
  11.2 0.1 compare_select_fusion.1
  11.3 0.1 reshape.232
  11.4 1.1 concatenate.3
  12.5 4.0 %gather_fusion.1 = bf16[1024,512]{1,0:T(8,128)(2,1)S(1)} fusion(bf16[513,512]{1,0:T(8,128)(2,1)S(1)} %concatenate.3, s32[1024]{0:T(1024)S(1)} %broadcast_clamp_fusion), kind=kCustom, calls=%fused_computation.1 | custom fusion | bytes 2101248 | tf_op jit(solution)/shard_map/jit(_take)/gather | solution.py:46
  16.4 0.0 copy-start.4
  16.4 0.0 copy-start.1
  16.5 1.2 broadcast_select_fusion
  17.6 11.5 %all-to-all-start = ((bf16[32,32,512]{2,1,0:T(8,128)(2,1)}), bf16[32,32,512]{2,1,0:T(8,128)(2,1)S(1)}, u32[]{:S(2)}, u32[]{:S(2)}) async-start(bf16[32,32,512]{2,1,0:T(8,128)(2,1)} %broadcast_select_fusion), calls=%async_computation.1 | async-start | bytes 2097152 | tf_op jit(solution)/shard_map/all_to_all | solution.py:53
  29.1 0.0 all-gather.3.cloned.1.call-start
  29.2 0.0 copy-done.4
  29.2 0.1 reshape.240
  29.3 0.0 copy-done.1
  29.3 0.0 copy-start.2
  29.3 6.8 %gather_fusion.2 = s32[1024]{0:T(1024)S(1)} fusion(s32[256]{0:T(256)S(1)} %copy-done.1, s32[1024]{0:T(1024)S(1)} %broadcast_clamp_fusion.1), kind=kCustom, calls=%fused_computation.2 | custom fusion | bytes 12288 | tf_op jit(solution)/shard_map/jit(_take)/gather | solution.py:33
  36.1 0.1 reshape.239
  36.2 0.1 fusion.16
  36.4 0.0 copy-done.2
  36.4 2.0 %gather_fusion.3 = bf16[32,512,64]{1,2,0:T(8,128)(2,1)} fusion(bf16[8,512,64]{1,2,0:T(8,128)(2,1)S(1)} %copy-done.2, s32[1024]{0:T(1024)S(1)} %pad_clamp_fusion.1), kind=kCustom, calls=%fused_computation.3 | custom fusion | bytes 4194432 | tf_op jit(solution)/shard_map/jit(_take)/gather | solution.py:36
  38.4 0.0 copy-start.3
  38.4 19.3 %all-to-all-done = bf16[32,32,512]{2,1,0:T(8,128)(2,1)S(1)} async-done(((bf16[32,32,512]{2,1,0:T(8,128)(2,1)}), bf16[32,32,512]{2,1,0:T(8,128)(2,1)S(1)}, u32[]{:S(2)}, u32[]{:S(2)}) %all-to-all-start) | async-done | bytes 1048608 | tf_op jit(solution)/shard_map/all_to_all | solution.py:53
  57.7 3.1 %fusion.10 = bf16[32,32,64]{2,1,0:T(8,128)(2,1)} fusion(bf16[32,32,512]{2,1,0:T(8,128)(2,1)S(1)} %all-to-all-done, bf16[32,512,64]{1,2,0:T(8,128)(2,1)} %gather_fusion.3, pred[32]{0:T(512)(128)(4,1)S(1)} %compare_and_fusion), kind=kOutput, calls=%fused_computation.17 | convolution fusion | flops 68222976 | bytes 3276832 | tf_op jit(solution)/shard_map/sdy,syj->sdj/dot_general | solution.py:51
  60.8 0.0 all-gather.3.cloned.1.call-update
  60.8 0.0 reduce-scatter.2.cloned.1.call-start
  60.9 0.0 copy-done.3
  60.9 10.1 %convolution_convert_fusion = bf16[512,8192]{1,0:T(8,128)(2,1)} fusion(bf16[512,512]{1,0:T(8,128)(2,1)S(1)} %copy-done.3, bf16[512,8192]{1,0:T(8,128)(2,1)} %param.10), kind=kOutput, calls=%fused_computation.6 | convolution fusion | flops 4299161600 | bytes 17301504 | tf_op jit(solution)/shard_map/dot_general | solution.py:47
  71.0 0.0 reduce-scatter.2.cloned.1.call-update
  71.0 0.0 copy-done
  71.0 2.8 %gather_fusion.4 = bf16[32,64,1024]{2,1,0:T(8,128)(2,1)} fusion(bf16[8,64,1024]{2,1,0:T(8,128)(2,1)S(1)} %copy-done, s32[1024]{0:T(1024)S(1)} %pad_clamp_fusion.1), kind=kCustom, calls=%fused_computation.4 | custom fusion | bytes 8388736 | tf_op jit(solution)/shard_map/jit(_take)/gather | solution.py:37
  73.8 10.3 %all-gather.3.cloned.1.call-done = bf16[256,32,64]{2,1,0:T(8,128)(2,1)} async-done(((bf16[32,32,64]{2,1,0:T(8,128)(2,1)}), bf16[256,32,64]{2,1,0:T(8,128)(2,1)}) %all-gather.3.cloned.1.call-update) | async-done | bytes 1048592 | tf_op jit(solution)/shard_map/all_gather | solution.py:58
  84.1 2.1 %reduce_sum.77 = bf16[32,32,64]{2,1,0:T(8,128)(2,1)S(1)} reduce(bf16[8,32,32,64]{3,2,1,0:T(8,128)(2,1)} %bitcast.37, bf16[]{:T(256)} %constant.133.clone.1), dimensions={0}, to_apply=%region_8.9 | reduce | flops 458752 | bytes 1179650 | tf_op jit(solution)/shard_map/reduce_sum | solution.py:57
  86.2 4.3 %fusion.7 = bf16[32,32,1024]{2,1,0:T(8,128)(2,1)} fusion(bf16[32,32,64]{2,1,0:T(8,128)(2,1)S(1)} %reduce_sum.77, bf16[32,64,1024]{2,1,0:T(8,128)(2,1)} %gather_fusion.4, pred[32]{0:T(512)(128)(4,1)S(1)} %compare_and_fusion), kind=kOutput, calls=%fused_computation.16 | convolution fusion | flops 137363456 | bytes 6422560 | tf_op jit(solution)/shard_map/iut,itb->iub/dot_general | solution.py:60
  90.6 9.8 %all-to-all-start.1 = ((bf16[32,32,1024]{2,1,0:T(8,128)(2,1)}), bf16[32,32,1024]{2,1,0:T(8,128)(2,1)S(1)}, u32[]{:S(2)}, u32[]{:S(2)}) async-start(bf16[32,32,1024]{2,1,0:T(8,128)(2,1)} %fusion.7), calls=%async_computation.2 | async-start | bytes 4194304 | tf_op jit(solution)/shard_map/all_to_all | solution.py:66
  100.4 0.1 convert_reduce_fusion
  100.5 0.1 select_reduce_fusion.1
  100.7 50.1 %all-to-all-done.1 = bf16[32,32,1024]{2,1,0:T(8,128)(2,1)S(1)} async-done(((bf16[32,32,1024]{2,1,0:T(8,128)(2,1)}), bf16[32,32,1024]{2,1,0:T(8,128)(2,1)S(1)}, u32[]{:S(2)}, u32[]{:S(2)}) %all-to-all-start.1) | async-done | bytes 2097184 | tf_op jit(solution)/shard_map/all_to_all | solution.py:66
  150.8 2.6 %bitcast_convert_fusion = f32[1024,1024]{1,0:T(8,128)} fusion(bf16[32,32,1024]{2,1,0:T(8,128)(2,1)S(1)} %all-to-all-done.1), kind=kLoop, calls=%fused_computation.10 | loop fusion | flops 1048576 | bytes 6291456 | tf_op jit(solution)/shard_map/reshape | solution.py:69
  153.4 5.0 %gather_fusion.5 = f32[512,1024]{1,0:T(8,128)S(1)} fusion(f32[1024,1024]{1,0:T(8,128)} %bitcast_convert_fusion, s32[1024]{0:T(1024)S(1)} %pad_clamp_fusion), kind=kCustom, calls=%fused_computation.5 | custom fusion | bytes 4196352 | tf_op jit(solution)/shard_map/jit(_take)/gather | solution.py:70
  158.4 0.0 reduce-scatter.2.cloned.1.call-done
  158.4 2.9 %add_convert_fusion = bf16[512,1024]{1,0:T(8,128)(2,1)} fusion(f32[512,1024]{1,0:T(8,128)S(1)} %gather_fusion.5, bf16[512,1024]{1,0:T(8,128)(2,1)} %reduce-scatter.2.cloned.1.call-done, bf16[512,1024]{1,0:T(8,128)(2,1)} %param.9, pred[512]{0:T(512)(128)(4,1)S(1)} %compare_and_fusion.1), kind=kLoop, calls=%fused_computation.11 | loop fusion | flops 3145728 | bytes 5243392 | tf_op jit(solution)/shard_map/convert_element_type | solution.py:71
  (11 shorter events, 0.1 us)
Async XLA Ops:
  6.5 64.5 %copy-start = (bf16[8,64,1024]{2,1,0:T(8,128)(2,1)S(1)}, bf16[8,64,1024]{2,1,0:T(8,128)(2,1)}, u32[]{:S(2)}) copy-start(bf16[8,64,1024]{2,1,0:T(8,128)(2,1)} %param.12) | copy-start | bytes 3145732
  16.4 12.7 %copy-start.4 = (s32[32,32]{1,0:T(8,128)S(1)}, s32[32,32]{1,0:T(8,128)}, u32[]{:S(2)}) copy-start(s32[32,32]{1,0:T(8,128)} %param.14) | copy-start | bytes 12292
  16.4 12.8 %copy-start.1 = (s32[256]{0:T(256)S(1)}, s32[256]{0:T(256)}, u32[]{:S(2)}) copy-start(s32[256]{0:T(256)} %param.13) | copy-start | bytes 3076
  17.6 40.1 %all-to-all-start = ((bf16[32,32,512]{2,1,0:T(8,128)(2,1)}), bf16[32,32,512]{2,1,0:T(8,128)(2,1)S(1)}, u32[]{:S(2)}, u32[]{:S(2)}) async-start(bf16[32,32,512]{2,1,0:T(8,128)(2,1)} %broadcast_select_fusion), calls=%async_computation.1 | async-start | bytes 2097152 | tf_op jit(solution)/shard_map/all_to_all | solution.py:53
  29.1 55.0 %all-gather.3.cloned.1.call-start = ((), (), s32[]{:S(2)}) async-start(), calls=%async_computation.4 | async-start | bytes 2359296 | tf_op jit(solution)/shard_map/all_gather | solution.py:58
  29.3 7.1 %copy-start.2 = (bf16[8,512,64]{1,2,0:T(8,128)(2,1)S(1)}, bf16[8,512,64]{1,2,0:T(8,128)(2,1)}, u32[]{:S(2)}) copy-start(bf16[8,512,64]{1,2,0:T(8,128)(2,1)} %param.11) | copy-start | bytes 1572868
  38.4 22.5 %copy-start.3 = (bf16[512,512]{1,0:T(8,128)(2,1)S(1)}, bf16[512,512]{1,0:T(8,128)(2,1)}, u32[]{:S(2)}) copy-start(bf16[512,512]{1,0:T(8,128)(2,1)} %param.8) | copy-start | bytes 1572868
  60.8 97.6 %reduce-scatter.2.cloned.1.call-start = ((), (), s32[]{:S(2)}) async-start(), calls=%async_computation.3 | async-start | bytes 9437184 | tf_op jit(solution)/shard_map/reduce_scatter | solution.py:48
  90.6 60.2 %all-to-all-start.1 = ((bf16[32,32,1024]{2,1,0:T(8,128)(2,1)}), bf16[32,32,1024]{2,1,0:T(8,128)(2,1)S(1)}, u32[]{:S(2)}, u32[]{:S(2)}) async-start(bf16[32,32,1024]{2,1,0:T(8,128)(2,1)} %fusion.7), calls=%async_computation.2 | async-start | bytes 4194304 | tf_op jit(solution)/shard_map/all_to_all | solution.py:66
Sparse Core Ops, SparseCore 0:
  61.0 23.1 all-gather.2
  86.7 54.7 reduce-scatter.1
